TPU v7x, 512 devices: a whole 4x4x16 slice. The times are simulated.
512 devices in a mesh: tm: 256 (over z, y, x), state: 2 (over core).
Axes of the slice: x: 4, y: 4, z: 16, core: 2. Of those that a mesh axis runs over, the one named last changes fastest.
Arguments:
- record: bfloat16 [32768, 4096], P('tm', 'state'), may hold values from -24 to 24
- gain: bfloat16 [2, 256, 4096], P(None, 'state'), may hold values from -0.0625 to 0.0625
- rate: float32 [256, 32768], P('state', 'tm'), as said below
- leak: float32 [256], P('state'), may hold values from 1.5258789e-05 to 0.05
- dilation: int32 [2], replicated, may hold values from 0 to 64, as said below
Outputs:
- smoothed: float32 [256, 32768], P('state', 'tm')
- grad: float32 [4096, 512], P(('state', 'tm'))
Inputs may be any that keep to these rules, and one draw needn't show every extreme that they name: `dilation`: delays of the taps; the largest of them equals 64. `rate`: positive rates.
All inputs are finite; a program needn't handle non-finite values.
Results may differ from a plain program's by a relative error of at most 0.0014.
Values may be sent and summed in bfloat16 or wider, within the bound.
No kernel may reach another device: no remote copies, remote signals or barrier semaphores. Data moves between devices by JAX's collectives and lax.ppermute only.
A program may use at most 64 MiB of HBM per device.

v0:
```python
import jax
import jax.numpy as jnp
from jax import lax
from jax.sharding import Mesh
from jax.sharding import PartitionSpec as P

TAPS = 2
DMAX = 64
TM = ("tm_0", "tm_1", "tm_2")
STATE_TM = ("state", "tm_0", "tm_1", "tm_2")


def from_behind(x, axis, by):
    peers = lax.axis_size(axis)
    pairs = [(i, i + by) for i in range(peers) if 0 <= i + by < peers]
    return lax.ppermute(x, axis, pairs)


def copy_for_each(x, axis):
    copies = jnp.broadcast_to(x, (lax.axis_size(axis), *x.shape))
    return lax.all_to_all(copies, axis, split_axis=0, concat_axis=0, tiled=True)


def of_everyone(x, axis):
    everything = copy_for_each(x, axis)
    return jnp.sum(everything, axis=0)


def laid_out(blocks, dim):
    blocks = jnp.moveaxis(blocks, 0, dim)
    lengths = blocks.shape
    return blocks.reshape(*lengths[:dim], lengths[dim] * lengths[dim + 1], *lengths[dim + 2 :])


def gathered_by_axis(x, axes, dim):
    far, near = axes
    blocks = copy_for_each(copy_for_each(x, far), near)
    return laid_out(blocks.swapaxes(0, 1).reshape(-1, *x.shape), dim)


def in_one_piece(arrays, axis, dim, along):
    widths = [a.shape[along] for a in arrays]
    both = jnp.concatenate(arrays, axis=along)
    whole = gathered_by_axis(both, axis, dim)
    return tuple(jnp.split(whole, [sum(widths[:k]) for k in range(1, len(widths))], axis=along))


def gather_directly(x, axis, dim):
    return laid_out(copy_for_each(x, axis), dim)


def in_blocks(x, dim, peers):
    lengths = x.shape
    blocks = x.reshape(*lengths[:dim], peers, lengths[dim] // peers, *lengths[dim + 1 :])
    return jnp.moveaxis(blocks, dim, 0)


def summed_on_arrival(x, axis, dim):
    peers = lax.axis_size(axis)
    blocks = lax.all_to_all(in_blocks(x, dim, peers), axis, 0, 0, tiled=True)
    return jnp.sum(blocks, axis=0)


def sum_by_axis(x, axes, dim):
    far, near = axes
    own = summed_on_arrival(in_blocks(x, dim, lax.axis_size(far)), near, dim + 1)
    return jnp.sum(lax.all_to_all(own, far, 0, 0, tiled=True), axis=0)


def affine(first, second):
    return (first[0] * second[0], second[0] * first[1] + second[1])


def entry_from_all(pair, backward, position, count):
    inclusive = lax.associative_scan(affine, pair, reverse=backward, axis=0)
    if backward:
        pick = position + 1
        valid = position < count - 1
    else:
        pick = position - 1
        valid = position > 0
    safe = jnp.clip(pick, 0, count - 1)
    value = lax.dynamic_index_in_dim(inclusive[1], safe, 0, keepdims=False)
    return jnp.where(valid, value, 0.0)


def running_sum(values, triangle):
    return jnp.dot(
        values, triangle, precision=lax.Precision.HIGHEST, preferred_element_type=jnp.float32
    )


def block_recursion(log_sums, inputs, keep):
    differ = jnp.where(keep[None], log_sums[:, :, None] - log_sums[:, None, :], 0.0)
    kernel = jnp.where(keep[None], jnp.exp(-jnp.abs(differ)), 0.0)
    return jnp.einsum(
        "hts,hs->ht",
        kernel,
        inputs,
        precision=lax.Precision.HIGHEST,
        preferred_element_type=jnp.float32,
    )


def per_device(record, gain, rate, leak, dilation):
    frames = record.shape[0]
    tail = record[frames - DMAX :]
    rim_rows = from_behind(tail, TM, 1)
    local_rows = jnp.concatenate([rim_rows, record], 0)
    local_taps = [
        lax.dynamic_slice_in_dim(local_rows, DMAX - dilation[k], frames, 0) for k in range(TAPS)
    ]
    gain_cols = lax.all_to_all(gain, "state", split_axis=2, concat_axis=1, tiled=True)
    local_view = jnp.stack(local_taps, 1)
    partial_drive = jnp.einsum(
        "lky,khy->hl", local_view, gain_cols, preferred_element_type=jnp.float32
    )
    total_drive = of_everyone(partial_drive, "state")
    own_modes = gain.shape[1]
    drive_in = lax.dynamic_slice_in_dim(
        total_drive, lax.axis_index("state") * own_modes, own_modes, 0
    )
    decay = jnp.exp(-rate)
    scale = jnp.sqrt(-jnp.expm1(-2.0 * rate))
    drive = scale * drive_in
    position = lax.axis_index(TM)
    count = lax.axis_size(TM)
    steps_idx = lax.iota(jnp.int32, frames)
    upper_incl = (steps_idx[:, None] <= steps_idx[None, :]).astype(jnp.float32)
    upper_excl = (steps_idx[:, None] < steps_idx[None, :]).astype(jnp.float32)
    lower_keep = steps_idx[:, None] >= steps_idx[None, :]
    upper_keep = steps_idx[:, None] <= steps_idx[None, :]
    rate_sums = running_sum(rate, upper_incl)
    offsets = block_recursion(rate_sums, drive, lower_keep)
    prods = jnp.exp(-rate_sums)
    summary = (prods[:, -1], offsets[:, -1])
    every = in_one_piece((summary[0][None], summary[1][None]), (("tm_0", "tm_1"), "tm_2"), 0, 1)
    entering = entry_from_all(every, False, position, count)
    filtered = prods * entering[:, None] + offsets
    kappa = 1.0 - leak
    weight = (1.0 - kappa[:, None] * decay * decay) * filtered
    link_rate = rate - jnp.log(kappa)[:, None]
    link_sums = running_sum(link_rate, upper_excl)
    weights = block_recursion(link_sums, weight, upper_keep)
    link_total = link_sums[:, -1:] + link_rate[:, -1:]
    links = jnp.exp(-(link_total - link_sums))
    closing = (links[:, 0], weights[:, 0])
    every_back = in_one_piece(
        (closing[0][None], closing[1][None]), (("tm_0", "tm_1"), "tm_2"), 0, 1
    )
    after = entry_from_all(every_back, True, position, count)
    smoothed = links * after[:, None] + weights
    prior = from_behind(smoothed[:, -1:], TM, 1)
    shifted = jnp.concatenate([prior, smoothed[:, :-1]], 1)
    resid = (smoothed - decay * shifted - drive).astype(jnp.bfloat16)
    resid_all = gather_directly(resid, "state", 0)
    pieces = []
    for k in range(TAPS):
        columns = local_taps[k]
        pieces.append(
            lax.dot_general(
                columns, resid_all, (((0,), (1,)), ((), ())), preferred_element_type=jnp.float32
            )
        )
    grad = sum_by_axis(jnp.concatenate(pieces, 1), (("tm_0", "tm_1"), "tm_2"), 0)
    return (smoothed, grad)


def solution(mesh):
    split = Mesh(
        mesh.devices.reshape(16, 4, 4, mesh.shape["state"]), ("tm_0", "tm_1", "tm_2", "state")
    )
    return jax.shard_map(
        per_device,
        mesh=split,
        in_specs=(P(TM, "state"), P(None, "state", None), P("state", TM), P("state"), P()),
        out_specs=(P("state", TM), P(STATE_TM, None)),
        check_vma=False,
    )
```

profile of v0, /device:TPU:8, one launch (start us, length us, event | category | flops | bytes accessed | tf_op | source)
XLA Modules:
  0.0 261.6 jit_solution(2452550016362452787)
XLA Ops:
  1.6 3.5 %collective-permute-start = (bf16[64,2048]{1,0:T(8,128)(2,1)S(1)}, bf16[64,2048]{1,0:T(8,128)(2,1)S(1)}, u32[]{:S(2)}, u32[]{:S(2)}) collective-permute-start(bf16[64,2048]{1,0:T(8,128)(2,1)S(1)} %slice.424), channel_id=1, source_target_pairs={{0,2},{2,4},{4,6},{6,8},{8,10},{10,12},{12,14},{14,16},{16,18},{18... | collective-permute-start | bytes 786440 | tf_op jit(solution)/shard_map/ppermute | solution.py:16
  5.2 6.2 %copy.67 = bf16[2,128,4096]{1,0,2:T(2,128)(2,1)} copy(bf16[2,128,4096]{2,1,0:T(8,128)(2,1)} %param.6) | data formatting | bytes 4194304 | tf_op args[1]
  11.3 3.9 %all-to-all-start = ((bf16[2,128,4096]{1,0,2:T(2,128)(2,1)}), bf16[2,128,4096]{1,0,2:T(2,128)(2,1)S(1)}, u32[]{:S(2)}, u32[]{:S(2)}) async-start(bf16[2,128,4096]{1,0,2:T(2,128)(2,1)} %copy.67), calls=%async_computation | async-start | bytes 4194304 | tf_op jit(solution)/shard_map/all_to_all | solution.py:113
  18.9 3.9 %copy.68 = bf16[2,128,2,2048]{3,1,2,0:T(8,128)(2,1)} copy(bf16[2,128,2,2048]{1,0,3,2:T(2,128)(2,1)S(1)} %bitcast.61) | data formatting | bytes 4194304 | tf_op jit(solution)/shard_map/all_to_all | solution.py:113
  25.7 3.9 %all_to_all.64 = f32[2,256,128]{2,1,0:T(8,128)S(1)} all-to-all(f32[2,256,128]{2,1,0:T(8,128)S(1)} %broadcast_in_dim.76), channel_id=1, replica_groups=mesh['tm_0'=16,'tm_1'=4,'tm_2'=4,'state'=2] {'state'}, dimensions={0} | all-to-all | bytes 524288 | tf_op jit(solution)/shard_map/all_to_all | solution.py:21
  30.0 4.7 %multiply_reduce_fusion.1 = f32[128,128]{1,0:T(8,128)S(1)} fusion(f32[128,128]{1,0:T(8,128)S(1)} %copy.91, f32[128,128]{1,0:T(8,128)S(1)} %copy.64, pred[128,128]{1,0:T(8,128)(4,1)S(1)} %iota_compare_fusion), kind=kLoop, calls=%fused_computation.1 | loop fusion | flops 14663680 | bytes 212992
  35.5 18.7 %all-to-all-start.2 = ((f32[64,1,256]{2,1,0:T(1,128)}), f32[64,1,256]{2,1,0:T(1,128)S(1)}, u32[]{:S(2)}, u32[]{:S(2)}) async-start(f32[64,1,256]{2,1,0:T(1,128)} %broadcast_in_dim.77), calls=%async_computation.2 | async-start | bytes 131072 | tf_op jit(solution)/shard_map/all_to_all | solution.py:21
  54.2 14.2 %all-to-all-done.2 = f32[64,1,256]{2,1,0:T(1,128)S(1)} async-done(((f32[64,1,256]{2,1,0:T(1,128)}), f32[64,1,256]{2,1,0:T(1,128)S(1)}, u32[]{:S(2)}, u32[]{:S(2)}) %all-to-all-start.2) | async-done | bytes 65568 | tf_op jit(solution)/shard_map/all_to_all | solution.py:21
  69.2 4.0 %all-to-all-start.3 = ((f32[4,64,1,256]{3,1,2,0:T(8,128)}), f32[4,64,1,256]{3,1,2,0:T(8,128)S(1)}, u32[]{:S(2)}, u32[]{:S(2)}) async-start(f32[4,64,1,256]{3,1,2,0:T(8,128)} %broadcast_in_dim.78), calls=%async_computation.3 | async-start | bytes 524288 | tf_op jit(solution)/shard_map/all_to_all | solution.py:21
  73.2 6.7 %all-to-all-done.3 = f32[4,64,1,256]{3,1,2,0:T(8,128)S(1)} async-done(((f32[4,64,1,256]{3,1,2,0:T(8,128)}), f32[4,64,1,256]{3,1,2,0:T(8,128)S(1)}, u32[]{:S(2)}, u32[]{:S(2)}) %all-to-all-start.3) | async-done | bytes 262176 | tf_op jit(solution)/shard_map/all_to_all | solution.py:21
  82.2 4.7 %multiply_reduce_fusion = f32[128,128]{1,0:T(8,128)S(1)} fusion(f32[128,128]{1,0:T(8,128)S(1)} %copy.92, f32[128,128]{1,0:T(8,128)S(1)} %copy.61, pred[128,128]{1,0:T(8,128)(4,1)S(1)} %iota_compare_fusion.1), kind=kLoop, calls=%fused_computation | loop fusion | flops 14663680 | bytes 212992
  87.0 19.1 %all_to_all.65 = f32[64,1,256]{2,1,0:T(1,128)S(1)} all-to-all(f32[64,1,256]{2,1,0:T(1,128)S(1)} %broadcast_in_dim.80), channel_id=1, replica_groups=mesh['tm_0'=16,'tm_1'=4,'tm_2'=4,'state'=2] {'tm_0','tm_1'}, dimensions={0} | all-to-all | bytes 131072 | tf_op jit(solution)/shard_map/all_to_all | solution.py:21
  106.8 3.4 %all-to-all-start.5 = ((f32[4,64,1,256]{3,1,2,0:T(8,128)}), f32[4,64,1,256]{3,1,2,0:T(8,128)S(1)}, u32[]{:S(2)}, u32[]{:S(2)}) async-start(f32[4,64,1,256]{3,1,2,0:T(8,128)} %broadcast_in_dim.81), calls=%async_computation.5 | async-start | bytes 524288 | tf_op jit(solution)/shard_map/all_to_all | solution.py:21
  110.3 6.6 %all-to-all-done.5 = f32[4,64,1,256]{3,1,2,0:T(8,128)S(1)} async-done(((f32[4,64,1,256]{3,1,2,0:T(8,128)}), f32[4,64,1,256]{3,1,2,0:T(8,128)S(1)}, u32[]{:S(2)}, u32[]{:S(2)}) %all-to-all-start.5) | async-done | bytes 262176 | tf_op jit(solution)/shard_map/all_to_all | solution.py:21
  118.9 2.5 collective-permute-start.1
  121.4 5.1 %collective-permute-done.1 = f32[128,1]{0,1:T(1,128)S(1)} collective-permute-done((f32[128,1]{0,1:T(1,128)S(1)}, f32[128,1]{0,1:T(1,128)S(1)}, u32[]{:S(2)}, u32[]{:S(2)}) %collective-permute-start.1) | collective-permute-done | bytes 544 | tf_op jit(solution)/shard_map/ppermute | solution.py:16
  126.7 3.8 %all_to_all.66 = bf16[2,128,128]{2,1,0:T(8,128)(2,1)S(1)} all-to-all(bf16[2,128,128]{2,1,0:T(8,128)(2,1)S(1)} %broadcast_in_dim.82), channel_id=1, replica_groups=mesh['tm_0'=16,'tm_1'=4,'tm_2'=4,'state'=2] {'state'}, dimensions={0} | all-to-all | bytes 131072 | tf_op jit(solution)/shard_map/all_to_all | solution.py:21
  131.3 2.4 pad_maximum_fusion
  133.8 5.4 %copy.74 = f32[2048,512]{1,0:T(8,128)} copy(f32[2048,512]{0,1:T(8,128)} %pad_maximum_fusion) | data formatting | bytes 8388608 | tf_op jit(solution)/shard_map/concatenate | solution.py:165
  139.2 2.8 %copy.75 = f32[4,64,8,512]{3,2,1,0:T(8,128)S(1)} copy(f32[4,64,8,512]{3,2,0,1:T(8,128)} %bitcast.60) | data formatting | bytes 8388608 | tf_op jit(solution)/shard_map/transpose | solution.py:55
  142.0 52.9 %all_to_all.67 = f32[4,64,8,512]{3,2,1,0:T(8,128)} all-to-all(f32[4,64,8,512]{3,2,1,0:T(8,128)S(1)} %copy.75), channel_id=1, replica_groups=mesh['tm_0'=16,'tm_1'=4,'tm_2'=4,'state'=2] {'tm_2'}, dimensions={0} | all-to-all | bytes 8388608 | tf_op jit(solution)/shard_map/all_to_all | solution.py:60
  194.9 3.8 %reduce_sum.28 = f32[64,8,512]{2,1,0:T(8,128)} reduce(f32[4,64,8,512]{3,2,1,0:T(8,128)} %all_to_all.67, f32[]{:T(128)} %constant.49.clone.1), dimensions={0}, to_apply=%region_1.2 | reduce | flops 786432 | bytes 5242884 | tf_op jit(solution)/shard_map/reduce_sum | solution.py:61
  198.7 7.5 %all-to-all-start.8 = ((f32[64,8,512]{2,1,0:T(8,128)}), f32[64,8,512]{2,1,0:T(8,128)S(1)}, u32[]{:S(2)}, u32[]{:S(2)}) async-start(f32[64,8,512]{2,1,0:T(8,128)} %reduce_sum.28), calls=%async_computation.8 | async-start | bytes 2097152 | tf_op jit(solution)/shard_map/all_to_all | solution.py:67
  206.9 54.0 %all-to-all-done.8 = f32[64,8,512]{2,1,0:T(8,128)S(1)} async-done(((f32[64,8,512]{2,1,0:T(8,128)}), f32[64,8,512]{2,1,0:T(8,128)S(1)}, u32[]{:S(2)}, u32[]{:S(2)}) %all-to-all-start.8) | async-done | bytes 1048608 | tf_op jit(solution)/shard_map/all_to_all | solution.py:67
  (251 shorter events, 13.3 us)
Async XLA Ops:
  1.6 13.6 %copy-start.2 = (s32[2]{0:T(128)S(1)}, s32[2]{0:T(128)}, u32[]{:S(2)}) copy-start(s32[2]{0:T(128)} %param.9) | copy-start | bytes 28
  1.6 16.8 %copy-start.1 = (f32[128,128]{1,0:T(8,128)S(1)}, f32[128,128]{1,0:T(8,128)}, u32[]{:S(2)}) copy-start(f32[128,128]{1,0:T(8,128)} %param.7) | copy-start | bytes 196612
  1.6 21.2 %collective-permute-start = (bf16[64,2048]{1,0:T(8,128)(2,1)S(1)}, bf16[64,2048]{1,0:T(8,128)(2,1)S(1)}, u32[]{:S(2)}, u32[]{:S(2)}) collective-permute-start(bf16[64,2048]{1,0:T(8,128)(2,1)S(1)} %slice.424), channel_id=1, source_target_pairs={{0,2},{2,4},{4,6},{6,8},{8,10},{10,12},{12,14},{14,16},{16,18},{18... | collective-permute-start | bytes 786440 | tf_op jit(solution)/shard_map/ppermute | solution.py:16
  11.3 11.5 %copy-start = (bf16[128,2048]{1,0:T(8,128)(2,1)S(1)}, bf16[128,2048]{1,0:T(8,128)(2,1)}, u32[]{:S(2)}) copy-start(bf16[128,2048]{1,0:T(8,128)(2,1)} %param.5) | copy-start | bytes 1572868
  11.3 7.6 %all-to-all-start = ((bf16[2,128,4096]{1,0,2:T(2,128)(2,1)}), bf16[2,128,4096]{1,0,2:T(2,128)(2,1)S(1)}, u32[]{:S(2)}, u32[]{:S(2)}) async-start(bf16[2,128,4096]{1,0,2:T(2,128)(2,1)} %copy.67), calls=%async_computation | async-start | bytes 4194304 | tf_op jit(solution)/shard_map/all_to_all | solution.py:113
  25.6 47.6 %copy-start.3 = (f32[128]{0:T(128)S(1)}, f32[128]{0:T(128)}, u32[]{:S(2)}) copy-start(f32[128]{0:T(128)} %param.8) | copy-start | bytes 1540
  35.5 33.0 %all-to-all-start.2 = ((f32[64,1,256]{2,1,0:T(1,128)}), f32[64,1,256]{2,1,0:T(1,128)S(1)}, u32[]{:S(2)}, u32[]{:S(2)}) async-start(f32[64,1,256]{2,1,0:T(1,128)} %broadcast_in_dim.77), calls=%async_computation.2 | async-start | bytes 131072 | tf_op jit(solution)/shard_map/all_to_all | solution.py:21
  69.2 10.7 %all-to-all-start.3 = ((f32[4,64,1,256]{3,1,2,0:T(8,128)}), f32[4,64,1,256]{3,1,2,0:T(8,128)S(1)}, u32[]{:S(2)}, u32[]{:S(2)}) async-start(f32[4,64,1,256]{3,1,2,0:T(8,128)} %broadcast_in_dim.78), calls=%async_computation.3 | async-start | bytes 524288 | tf_op jit(solution)/shard_map/all_to_all | solution.py:21
  106.8 10.1 %all-to-all-start.5 = ((f32[4,64,1,256]{3,1,2,0:T(8,128)}), f32[4,64,1,256]{3,1,2,0:T(8,128)S(1)}, u32[]{:S(2)}, u32[]{:S(2)}) async-start(f32[4,64,1,256]{3,1,2,0:T(8,128)} %broadcast_in_dim.81), calls=%async_computation.5 | async-start | bytes 524288 | tf_op jit(solution)/shard_map/all_to_all | solution.py:21
  118.9 7.5 %collective-permute-start.1 = (f32[128,1]{0,1:T(1,128)S(1)}, f32[128,1]{0,1:T(1,128)S(1)}, u32[]{:S(2)}, u32[]{:S(2)}) collective-permute-start(f32[128,1]{0,1:T(1,128)S(1)} %slice.587), channel_id=1, source_target_pairs={{0,2},{2,4},{4,6},{6,8},{8,10},{10,12},{12,14},{14,16},{16,18},{18... | collective-permute-start | bytes 1544 | tf_op jit(solution)/shard_map/ppermute | solution.py:16
  198.7 62.2 %all-to-all-start.8 = ((f32[64,8,512]{2,1,0:T(8,128)}), f32[64,8,512]{2,1,0:T(8,128)S(1)}, u32[]{:S(2)}, u32[]{:S(2)}) async-start(f32[64,8,512]{2,1,0:T(8,128)} %reduce_sum.28), calls=%async_computation.8 | async-start | bytes 2097152 | tf_op jit(solution)/shard_map/all_to_all | solution.py:67
where the time goes:
time: 263 us; the launch traced here: 262 us
  waiting for transfers between devices  86.6 us (33%)
  blocking collectives  79.7 us (30%)
  starting transfers between devices  43.5 us (17%)
  local copies, waits for them, and re-layouts  26.3 us (10%)
  other arithmetic  17.2 us (7%)
  between operations  4.56 us (2%)
  matrix products  3.8 us (1%)
    all_to_all x1, waiting for transfers between devices, sum_by_axis(): return jnp.sum(lax.all_to_all(own, far, 0, 0, tiled=True), axis=0)  54 us
    all_to_all x1, blocking collectives, summed_on_arrival(): blocks = lax.all_to_all(in_blocks(x, dim, peers), axis, 0, 0, tiled=True)  52.9 us
    all_to_all x3, waiting for transfers between devices, copy_for_each(): return lax.all_to_all(copies, axis, split_axis=0, concat_axis=0, tiled=True)  27.5 us
    all_to_all x3, blocking collectives, copy_for_each(): return lax.all_to_all(copies, axis, split_axis=0, concat_axis=0, tiled=True)  26.8 us
    all_to_all x3, starting transfers between devices, copy_for_each(): return lax.all_to_all(copies, axis, split_axis=0, concat_axis=0, tiled=True)  26.1 us
    unnamed x2, other arithmetic  9.43 us
    all_to_all x1, starting transfers between devices, sum_by_axis(): return jnp.sum(lax.all_to_all(own, far, 0, 0, tiled=True), axis=0)  7.47 us
    unnamed x17, local copies, waits for them, and re-layouts  7.29 us
  transfers between devices with their start and end apart: 7, of which 5 were waited for; matrix products, arithmetic and copies ran while one was open for 5% of the time, Pallas kernels for 0%

commit v1 on v0

--- a/solution.py
+++ b/solution.py
@@ -110,7 +110,10 @@
     local_taps = [
         lax.dynamic_slice_in_dim(local_rows, DMAX - dilation[k], frames, 0) for k in range(TAPS)
     ]
-    gain_cols = lax.all_to_all(gain, "state", split_axis=2, concat_axis=1, tiled=True)
+    gain_cols = jnp.concatenate(
+        lax.all_to_all(jnp.stack(jnp.split(gain, lax.axis_size("state"), axis=2)), "state", 0, 0),
+        axis=1,
+    )
     local_view = jnp.stack(local_taps, 1)
     partial_drive = jnp.einsum(
         "lky,khy->hl", local_view, gain_cols, preferred_element_type=jnp.float32

time: 263 us -> 257 us (0.977)
  local copies, waits for them, and re-layouts: 26.3 us -> 19.3 us
    unnamed x17 -> x16, local copies, waits for them, and re-layouts: 7.29 us -> 1.14 us
    all_to_all x1 -> x0, local copies, waits for them, and re-layouts: 3.88 us -> none  [per_device(): lax.all_to_all(gain, 'state', split_axis=2, concat_axis=1, tiled=True)]
  transfers between devices with their start and end apart: 7 -> 7, of which waited for: 5 -> 5; matrix products, arithmetic and copies ran while one was open for 5% -> 3% of each run, Pallas kernels for 0% -> 0%
where the time goes in v1:
time: 257 us; the launch traced here: 256 us
  waiting for transfers between devices  86.6 us (34%)
  blocking collectives  79.7 us (31%)
  starting transfers between devices  43.4 us (17%)
  local copies, waits for them, and re-layouts  19.3 us (8%)
  other arithmetic  18.7 us (7%)
  between operations  4.55 us (2%)
  matrix products  3.68 us (1%)
    all_to_all x1, waiting for transfers between devices, sum_by_axis(): return jnp.sum(lax.all_to_all(own, far, 0, 0, tiled=True), axis=0)  54 us
    all_to_all x1, blocking collectives, summed_on_arrival(): blocks = lax.all_to_all(in_blocks(x, dim, peers), axis, 0, 0, tiled=True)  52.9 us
    all_to_all x3, waiting for transfers between devices, copy_for_each(): return lax.all_to_all(copies, axis, split_axis=0, concat_axis=0, tiled=True)  27.5 us
    all_to_all x3, blocking collectives, copy_for_each(): return lax.all_to_all(copies, axis, split_axis=0, concat_axis=0, tiled=True)  26.8 us
    all_to_all x3, starting transfers between devices, copy_for_each(): return lax.all_to_all(copies, axis, split_axis=0, concat_axis=0, tiled=True)  26.1 us
    unnamed x2, other arithmetic  9.43 us
    all_to_all x1, starting transfers between devices, sum_by_axis(): return jnp.sum(lax.all_to_all(own, far, 0, 0, tiled=True), axis=0)  7.47 us
    ppermute x2, starting transfers between devices, from_behind(): return lax.ppermute(x, axis, pairs)  5.87 us
  transfers between devices with their start and end apart: 7, of which 5 were waited for; matrix products, arithmetic and copies ran while one was open for 3% of the time, Pallas kernels for 0%

profile of v1, /device:TPU:8, one launch (start us, length us, event | category | flops | bytes accessed | tf_op | source)
XLA Modules:
  0.0 255.9 jit_solution(9385085939151351410)
XLA Ops:
  1.6 3.4 %collective-permute-start = (bf16[64,2048]{1,0:T(8,128)(2,1)S(1)}, bf16[64,2048]{1,0:T(8,128)(2,1)S(1)}, u32[]{:S(2)}, u32[]{:S(2)}) collective-permute-start(bf16[64,2048]{1,0:T(8,128)(2,1)S(1)} %slice.424), channel_id=1, source_target_pairs={{0,2},{2,4},{4,6},{6,8},{8,10},{10,12},{12,14},{14,16},{16,18},{18... | collective-permute-start | bytes 786440 | tf_op jit(solution)/shard_map/ppermute | solution.py:16
  5.0 1.7 slice_bitcast_fusion.1
  8.2 3.9 %all-to-all-start = ((bf16[2,2,128,2048]{3,2,1,0:T(8,128)(2,1)}), bf16[2,2,128,2048]{3,2,1,0:T(8,128)(2,1)S(1)}, u32[]{:S(2)}, u32[]{:S(2)}) async-start(bf16[2,2,128,2048]{3,2,1,0:T(8,128)(2,1)} %pad_maximum_fusion.1), calls=%async_computation | async-start | bytes 4194304 | tf_op jit(solution)/shard_map/all_to_all | solution.py:114
  17.7 2.3 convolution_bitcast_fusion
  20.0 3.9 %all_to_all.51 = f32[2,256,128]{2,1,0:T(8,128)S(1)} all-to-all(f32[2,256,128]{2,1,0:T(8,128)S(1)} %broadcast_in_dim.76), channel_id=1, replica_groups=mesh['tm_0'=16,'tm_1'=4,'tm_2'=4,'state'=2] {'state'}, dimensions={0} | all-to-all | bytes 524288 | tf_op jit(solution)/shard_map/all_to_all | solution.py:21
  24.3 4.7 %multiply_reduce_fusion.1 = f32[128,128]{1,0:T(8,128)S(1)} fusion(f32[128,128]{1,0:T(8,128)S(1)} %copy.83, f32[128,128]{1,0:T(8,128)S(1)} %copy.58, pred[128,128]{1,0:T(8,128)(4,1)S(1)} %iota_compare_fusion), kind=kLoop, calls=%fused_computation.1 | loop fusion | flops 14663680 | bytes 212992
  29.8 18.7 %all-to-all-start.2 = ((f32[64,1,256]{2,1,0:T(1,128)}), f32[64,1,256]{2,1,0:T(1,128)S(1)}, u32[]{:S(2)}, u32[]{:S(2)}) async-start(f32[64,1,256]{2,1,0:T(1,128)} %broadcast_in_dim.77), calls=%async_computation.2 | async-start | bytes 131072 | tf_op jit(solution)/shard_map/all_to_all | solution.py:21
  48.5 14.2 %all-to-all-done.2 = f32[64,1,256]{2,1,0:T(1,128)S(1)} async-done(((f32[64,1,256]{2,1,0:T(1,128)}), f32[64,1,256]{2,1,0:T(1,128)S(1)}, u32[]{:S(2)}, u32[]{:S(2)}) %all-to-all-start.2) | async-done | bytes 65568 | tf_op jit(solution)/shard_map/all_to_all | solution.py:21
  63.5 4.0 %all-to-all-start.3 = ((f32[4,64,1,256]{3,1,2,0:T(8,128)}), f32[4,64,1,256]{3,1,2,0:T(8,128)S(1)}, u32[]{:S(2)}, u32[]{:S(2)}) async-start(f32[4,64,1,256]{3,1,2,0:T(8,128)} %broadcast_in_dim.78), calls=%async_computation.3 | async-start | bytes 524288 | tf_op jit(solution)/shard_map/all_to_all | solution.py:21
  67.5 6.7 %all-to-all-done.3 = f32[4,64,1,256]{3,1,2,0:T(8,128)S(1)} async-done(((f32[4,64,1,256]{3,1,2,0:T(8,128)}), f32[4,64,1,256]{3,1,2,0:T(8,128)S(1)}, u32[]{:S(2)}, u32[]{:S(2)}) %all-to-all-start.3) | async-done | bytes 262176 | tf_op jit(solution)/shard_map/all_to_all | solution.py:21
  76.5 4.7 %multiply_reduce_fusion = f32[128,128]{1,0:T(8,128)S(1)} fusion(f32[128,128]{1,0:T(8,128)S(1)} %copy.84, f32[128,128]{1,0:T(8,128)S(1)} %copy.55, pred[128,128]{1,0:T(8,128)(4,1)S(1)} %iota_compare_fusion.1), kind=kLoop, calls=%fused_computation | loop fusion | flops 14663680 | bytes 212992
  81.4 19.1 %all_to_all.52 = f32[64,1,256]{2,1,0:T(1,128)S(1)} all-to-all(f32[64,1,256]{2,1,0:T(1,128)S(1)} %broadcast_in_dim.80), channel_id=1, replica_groups=mesh['tm_0'=16,'tm_1'=4,'tm_2'=4,'state'=2] {'tm_0','tm_1'}, dimensions={0} | all-to-all | bytes 131072 | tf_op jit(solution)/shard_map/all_to_all | solution.py:21
  101.2 3.4 %all-to-all-start.5 = ((f32[4,64,1,256]{3,1,2,0:T(8,128)}), f32[4,64,1,256]{3,1,2,0:T(8,128)S(1)}, u32[]{:S(2)}, u32[]{:S(2)}) async-start(f32[4,64,1,256]{3,1,2,0:T(8,128)} %broadcast_in_dim.81), calls=%async_computation.5 | async-start | bytes 524288 | tf_op jit(solution)/shard_map/all_to_all | solution.py:21
  104.6 6.6 %all-to-all-done.5 = f32[4,64,1,256]{3,1,2,0:T(8,128)S(1)} async-done(((f32[4,64,1,256]{3,1,2,0:T(8,128)}), f32[4,64,1,256]{3,1,2,0:T(8,128)S(1)}, u32[]{:S(2)}, u32[]{:S(2)}) %all-to-all-start.5) | async-done | bytes 262176 | tf_op jit(solution)/shard_map/all_to_all | solution.py:21
  113.3 2.5 collective-permute-start.1
  115.7 5.1 %collective-permute-done.1 = f32[128,1]{0,1:T(1,128)S(1)} collective-permute-done((f32[128,1]{0,1:T(1,128)S(1)}, f32[128,1]{0,1:T(1,128)S(1)}, u32[]{:S(2)}, u32[]{:S(2)}) %collective-permute-start.1) | collective-permute-done | bytes 544 | tf_op jit(solution)/shard_map/ppermute | solution.py:16
  121.0 3.8 %all_to_all.53 = bf16[2,128,128]{2,1,0:T(8,128)(2,1)S(1)} all-to-all(bf16[2,128,128]{2,1,0:T(8,128)(2,1)S(1)} %broadcast_in_dim.82), channel_id=1, replica_groups=mesh['tm_0'=16,'tm_1'=4,'tm_2'=4,'state'=2] {'state'}, dimensions={0} | all-to-all | bytes 131072 | tf_op jit(solution)/shard_map/all_to_all | solution.py:21
  125.7 2.4 pad_maximum_fusion
  128.1 5.5 %copy.66 = f32[2048,512]{1,0:T(8,128)} copy(f32[2048,512]{0,1:T(8,128)} %pad_maximum_fusion) | data formatting | bytes 8388608 | tf_op jit(solution)/shard_map/concatenate | solution.py:168
  133.6 2.8 %copy.67 = f32[4,64,8,512]{3,2,1,0:T(8,128)S(1)} copy(f32[4,64,8,512]{3,2,0,1:T(8,128)} %bitcast.60) | data formatting | bytes 8388608 | tf_op jit(solution)/shard_map/transpose | solution.py:55
  136.4 52.9 %all_to_all.54 = f32[4,64,8,512]{3,2,1,0:T(8,128)} all-to-all(f32[4,64,8,512]{3,2,1,0:T(8,128)S(1)} %copy.67), channel_id=1, replica_groups=mesh['tm_0'=16,'tm_1'=4,'tm_2'=4,'state'=2] {'tm_2'}, dimensions={0} | all-to-all | bytes 8388608 | tf_op jit(solution)/shard_map/all_to_all | solution.py:60
  189.3 3.8 %reduce_sum.28 = f32[64,8,512]{2,1,0:T(8,128)} reduce(f32[4,64,8,512]{3,2,1,0:T(8,128)} %all_to_all.54, f32[]{:T(128)} %constant.49.clone.1), dimensions={0}, to_apply=%region_1.2 | reduce | flops 786432 | bytes 5242884 | tf_op jit(solution)/shard_map/reduce_sum | solution.py:61
  193.0 7.5 %all-to-all-start.8 = ((f32[64,8,512]{2,1,0:T(8,128)}), f32[64,8,512]{2,1,0:T(8,128)S(1)}, u32[]{:S(2)}, u32[]{:S(2)}) async-start(f32[64,8,512]{2,1,0:T(8,128)} %reduce_sum.28), calls=%async_computation.8 | async-start | bytes 2097152 | tf_op jit(solution)/shard_map/all_to_all | solution.py:67
  201.3 54.0 %all-to-all-done.8 = f32[64,8,512]{2,1,0:T(8,128)S(1)} async-done(((f32[64,8,512]{2,1,0:T(8,128)}), f32[64,8,512]{2,1,0:T(8,128)S(1)}, u32[]{:S(2)}, u32[]{:S(2)}) %all-to-all-start.8) | async-done | bytes 1048608 | tf_op jit(solution)/shard_map/all_to_all | solution.py:67
  (251 shorter events, 13.9 us)
Async XLA Ops:
  1.6 15.7 %collective-permute-start = (bf16[64,2048]{1,0:T(8,128)(2,1)S(1)}, bf16[64,2048]{1,0:T(8,128)(2,1)S(1)}, u32[]{:S(2)}, u32[]{:S(2)}) collective-permute-start(bf16[64,2048]{1,0:T(8,128)(2,1)S(1)} %slice.424), channel_id=1, source_target_pairs={{0,2},{2,4},{4,6},{6,8},{8,10},{10,12},{12,14},{14,16},{16,18},{18... | collective-permute-start | bytes 786440 | tf_op jit(solution)/shard_map/ppermute | solution.py:16
  6.7 5.5 %copy-start.2 = (s32[2]{0:T(128)S(1)}, s32[2]{0:T(128)}, u32[]{:S(2)}) copy-start(s32[2]{0:T(128)} %param.9) | copy-start | bytes 28
  6.7 8.6 %copy-start.1 = (f32[128,128]{1,0:T(8,128)S(1)}, f32[128,128]{1,0:T(8,128)}, u32[]{:S(2)}) copy-start(f32[128,128]{1,0:T(8,128)} %param.7) | copy-start | bytes 196612
  8.2 9.1 %copy-start = (bf16[128,2048]{1,0:T(8,128)(2,1)S(1)}, bf16[128,2048]{1,0:T(8,128)(2,1)}, u32[]{:S(2)}) copy-start(bf16[128,2048]{1,0:T(8,128)(2,1)} %param.5) | copy-start | bytes 1572868
  8.2 7.6 %all-to-all-start = ((bf16[2,2,128,2048]{3,2,1,0:T(8,128)(2,1)}), bf16[2,2,128,2048]{3,2,1,0:T(8,128)(2,1)S(1)}, u32[]{:S(2)}, u32[]{:S(2)}) async-start(bf16[2,2,128,2048]{3,2,1,0:T(8,128)(2,1)} %pad_maximum_fusion.1), calls=%async_computation | async-start | bytes 4194304 | tf_op jit(solution)/shard_map/all_to_all | solution.py:114
  20.0 47.5 %copy-start.3 = (f32[128]{0:T(128)S(1)}, f32[128]{0:T(128)}, u32[]{:S(2)}) copy-start(f32[128]{0:T(128)} %param.8) | copy-start | bytes 1540
  29.8 33.0 %all-to-all-start.2 = ((f32[64,1,256]{2,1,0:T(1,128)}), f32[64,1,256]{2,1,0:T(1,128)S(1)}, u32[]{:S(2)}, u32[]{:S(2)}) async-start(f32[64,1,256]{2,1,0:T(1,128)} %broadcast_in_dim.77), calls=%async_computation.2 | async-start | bytes 131072 | tf_op jit(solution)/shard_map/all_to_all | solution.py:21
  63.5 10.7 %all-to-all-start.3 = ((f32[4,64,1,256]{3,1,2,0:T(8,128)}), f32[4,64,1,256]{3,1,2,0:T(8,128)S(1)}, u32[]{:S(2)}, u32[]{:S(2)}) async-start(f32[4,64,1,256]{3,1,2,0:T(8,128)} %broadcast_in_dim.78), calls=%async_computation.3 | async-start | bytes 524288 | tf_op jit(solution)/shard_map/all_to_all | solution.py:21
  101.2 10.1 %all-to-all-start.5 = ((f32[4,64,1,256]{3,1,2,0:T(8,128)}), f32[4,64,1,256]{3,1,2,0:T(8,128)S(1)}, u32[]{:S(2)}, u32[]{:S(2)}) async-start(f32[4,64,1,256]{3,1,2,0:T(8,128)} %broadcast_in_dim.81), calls=%async_computation.5 | async-start | bytes 524288 | tf_op jit(solution)/shard_map/all_to_all | solution.py:21
  113.3 7.5 %collective-permute-start.1 = (f32[128,1]{0,1:T(1,128)S(1)}, f32[128,1]{0,1:T(1,128)S(1)}, u32[]{:S(2)}, u32[]{:S(2)}) collective-permute-start(f32[128,1]{0,1:T(1,128)S(1)} %slice.587), channel_id=1, source_target_pairs={{0,2},{2,4},{4,6},{6,8},{8,10},{10,12},{12,14},{14,16},{16,18},{18... | collective-permute-start | bytes 1544 | tf_op jit(solution)/shard_map/ppermute | solution.py:16
  193.0 62.2 %all-to-all-start.8 = ((f32[64,8,512]{2,1,0:T(8,128)}), f32[64,8,512]{2,1,0:T(8,128)S(1)}, u32[]{:S(2)}, u32[]{:S(2)}) async-start(f32[64,8,512]{2,1,0:T(8,128)} %reduce_sum.28), calls=%async_computation.8 | async-start | bytes 2097152 | tf_op jit(solution)/shard_map/all_to_all | solution.py:67
